TPU v7x, 32 devices: a whole 2x2x4 slice. The times are simulated.
32 devices in a mesh: row: 8 (over y, x, core), col: 4 (over z).
Axes of the slice: x: 2, y: 2, z: 4, core: 2. Of those that a mesh axis runs over, the one named last changes fastest.
Arguments:
- tile_values: bfloat16 [8, 4, 64, 128, 128], P('row', 'col'), may hold values from -0.0625 to 0.0625
- tile_row: int32 [8, 4, 64], P('row', 'col'), may hold values from 0 to 3
- tile_col: int32 [8, 4, 64], P('row', 'col'), may hold values from 0 to 3
- tile_count: int32 [8, 4], P('row', 'col'), may hold values from 16 to 64, as said below
- primal_init: float32 [64, 2048], P(None, ('row', 'col')), may hold values from -3 to 3
- dual_init: float32 [64, 4096], P(None, ('row', 'col')), may hold values from -3 to 3
- cost_vector: float32 [2048], P(('row', 'col')), may hold values from -4 to 4
- lower_bound: float32 [2048], P(('row', 'col')), may hold values from -1 to -0.2
- upper_bound: float32 [2048], P(('row', 'col')), may hold values from 0.2 to 1
- bound_kind: int32 [2048], P(('row', 'col')), may hold values from 0 to 2
- row_kind: int32 [4096], P(('row', 'col')), may hold values from 0 to 1
- demand: float32 [64, 4096], P(None, ('row', 'col')), may hold values from -20 to 20
Outputs:
- primal_out: float32 [64, 2048], P(None, ('row', 'col'))
- dual_out: float32 [64, 4096], P(None, ('row', 'col'))
- residual_norm: float32 [3, 64], replicated
Inputs may be any that keep to these rules, and one draw needn't show every extreme that they name: `tile_count`: live tile slots of one device; some device has all 64 slots live.
All inputs are finite; a program needn't handle non-finite values.
Results may differ from a plain program's by a relative error of at most 0.0022.
Values may be sent and summed in bfloat16 or wider, within the bound.
A program may use at most 64 MiB of HBM per device.

v0:
```python
import jax
import jax.numpy as jnp
from jax import lax
from jax.sharding import PartitionSpec as P

ITERS = 3


PRIMAL_STEP = 0.4
DUAL_STEP = 0.4
NORM_EPS = 1e-06


def block_sum(onehot, product):
    return jnp.einsum("tr,sti->sri", onehot, product, precision=lax.Precision.HIGHEST)


def shards(
    tile_values,
    tile_row,
    tile_col,
    tile_count,
    primal_init,
    dual_init,
    cost_vector,
    lower_bound,
    upper_bound,
    bound_kind,
    row_kind,
    demand,
):
    blocks = tile_values[0, 0]
    slot_rows = tile_row[0, 0]
    slot_cols = tile_col[0, 0]
    live_count = tile_count[0, 0]
    slots = blocks.shape[0]
    tile_size = blocks.shape[-1]
    scenarios = primal_init.shape[0]
    row_devices = lax.axis_size("row")
    col_devices = lax.axis_size("col")
    col_blocks = row_devices // 2
    live_mask = jnp.arange(slots, dtype=jnp.int32) < live_count
    row_onehot = (
        (slot_rows[:, None] == jnp.arange(col_devices, dtype=jnp.int32)[None, :])
        & live_mask[:, None]
    ).astype(jnp.float32)
    col_onehot = (
        (slot_cols[:, None] == jnp.arange(col_blocks, dtype=jnp.int32)[None, :])
        & live_mask[:, None]
    ).astype(jnp.float32)
    total_rows = row_devices * col_devices * tile_size
    inequality = (row_kind == 1).astype(jnp.float32)
    primal = primal_init
    dual = dual_init
    partial_norms = []
    for iteration in range(ITERS):
        dual_half = lax.all_gather(dual.astype(jnp.bfloat16), "col", axis=1, tiled=True)
        grouped = dual_half.reshape(scenarios, col_devices, tile_size)
        picked = jnp.take(grouped, slot_rows, axis=1)
        product = jnp.einsum("tij,sti->stj", blocks, picked, preferred_element_type=jnp.float32)
        summed = block_sum(col_onehot, product)
        summed = summed.reshape(scenarios, col_blocks * tile_size)
        transposed = lax.psum_scatter(summed, "row", scatter_dimension=1, tiled=True)
        primal_next = primal - PRIMAL_STEP * (cost_vector[None, :] - transposed)
        primal_next = jnp.where(
            (bound_kind <= 1)[None, :], jnp.maximum(primal_next, lower_bound[None, :]), primal_next
        )
        primal_next = jnp.where(
            (bound_kind == 0)[None, :], jnp.minimum(primal_next, upper_bound[None, :]), primal_next
        )
        extrapolated = (2.0 * primal_next - primal).astype(jnp.bfloat16)
        gathered = lax.all_gather(extrapolated, "row", axis=1, tiled=True)
        apply_grouped = gathered.reshape(scenarios, col_blocks, tile_size)
        apply_picked = jnp.take(apply_grouped, slot_cols, axis=1)
        apply_product = jnp.einsum(
            "tij,stj->sti", blocks, apply_picked, preferred_element_type=jnp.float32
        )
        apply_summed = block_sum(row_onehot, apply_product)
        partial_value = apply_summed.reshape(scenarios, col_devices * tile_size)
        image = lax.psum_scatter(partial_value, "col", scatter_dimension=1, tiled=True)
        gap_rows = demand - image
        dual = dual + DUAL_STEP * gap_rows
        dual = jnp.where(inequality[None, :] > 0.0, jnp.maximum(dual, 0.0), dual)
        primal = primal_next
        squares = jnp.sum(gap_rows * gap_rows, axis=1)
        partial_norms.append(lax.psum(squares, ("row", "col")))
    totals = jnp.stack(partial_norms)
    residual_norm = jnp.sqrt(totals / total_rows + NORM_EPS)
    return (primal, dual, residual_norm)


def solution(mesh):
    return jax.shard_map(
        shards,
        mesh=mesh,
        in_specs=(
            P("row", "col", None, None, None),
            P("row", "col", None),
            P("row", "col", None),
            P("row", "col"),
            P(None, ("row", "col")),
            P(None, ("row", "col")),
            P(("row", "col")),
            P(("row", "col")),
            P(("row", "col")),
            P(("row", "col")),
            P(("row", "col")),
            P(None, ("row", "col")),
        ),
        out_specs=(P(None, ("row", "col")), P(None, ("row", "col")), P()),
        check_vma=False,
    )
```

profile of v0, /device:TPU:0, one launch (start us, length us, event | category | flops | bytes accessed | tf_op | source)
XLA Modules:
  0.0 312.4 jit_solution(8858715847128932885)
XLA Ops:
  7.2 0.0 reduce-scatter.19.cloned.1.call-start
  7.2 0.8 compare_and_fusion.1
  8.0 0.7 compare_select_fusion.1
  9.4 0.8 convert_element_type.23
  10.1 13.7 %all_gather.18 = bf16[64,512]{1,0:T(8,128)(2,1)S(1)} all-gather(bf16[64,128]{1,0:T(8,128)(2,1)S(1)} %convert_element_type.23), channel_id=1, replica_groups=mesh['row'=8,'col'=4] {'col'}, dimensions={1}, use_global_device_ids=true | all-gather | bytes 81920 | tf_op jit(solution)/shard_map/all_gather | solution.py:57
  23.8 0.7 gather_fusion
  24.6 0.7 fusion.24
  25.4 2.0 fusion.42
  27.3 0.8 copy.57
  28.2 0.0 reduce-scatter.19.cloned.1.call-update
  28.2 0.0 reduce-scatter.13.cloned.1.call-start
  28.3 33.6 %reduce-scatter.19.cloned.1.call-done = f32[64,64]{1,0:T(8,128)} async-done(((f32[512,64]{1,0:T(8,128)}), f32[64,64]{1,0:T(8,128)}) %reduce-scatter.19.cloned.1.call-update) | async-done | bytes 16400
  61.9 0.8 copy.52
  62.8 0.1 copy.29
  62.9 9.2 %all_gather.19 = bf16[64,512]{0,1:T(8,128)(2,1)S(1)} all-gather(bf16[64,64]{0,1:T(8,128)(2,1)S(1)} %copy.29), channel_id=1, replica_groups=mesh['row'=8,'col'=4] {'row'}, dimensions={1}, use_global_device_ids=true | all-gather | bytes 73728 | tf_op jit(solution)/shard_map/all_gather | solution.py:72
  72.1 0.1 copy.31
  72.2 0.8 gather_fusion.1
  73.0 1.5 fusion.27
  74.5 2.0 fusion.20
  76.5 0.7 copy.92
  77.2 0.0 reduce-scatter.13.cloned.1.call-update
  77.2 0.0 reduce-scatter.21.cloned.1.call-start
  77.3 19.3 %reduce-scatter.13.cloned.1.call-done = f32[64,128]{1,0:T(8,128)} async-done(((f32[64,512]{1,0:T(8,128)}), f32[64,128]{1,0:T(8,128)}) %reduce-scatter.13.cloned.1.call-update) | async-done | bytes 32784 | tf_op jit(solution)/shard_map/reduce_scatter | solution.py:80
  96.5 0.8 fusion.75
  97.3 12.0 %all_gather.20 = bf16[64,512]{1,0:T(8,128)(2,1)S(1)} all-gather(bf16[64,128]{1,0:T(8,128)(2,1)S(1)} %fusion.75), channel_id=1, replica_groups=mesh['row'=8,'col'=4] {'col'}, dimensions={1}, use_global_device_ids=true | all-gather | bytes 81920 | tf_op jit(solution)/shard_map/all_gather | solution.py:57
  109.3 0.7 gather_fusion.2
  110.1 0.7 fusion.30
  110.8 2.0 fusion.45
  112.7 0.8 copy.58
  113.6 0.0 reduce-scatter.21.cloned.1.call-update
  113.6 0.0 reduce-scatter.15.cloned.1.call-start
  113.7 32.2 %reduce-scatter.21.cloned.1.call-done = f32[64,64]{1,0:T(8,128)} async-done(((f32[512,64]{1,0:T(8,128)}), f32[64,64]{1,0:T(8,128)}) %reduce-scatter.21.cloned.1.call-update) | async-done | bytes 16400
  145.8 0.8 copy.54
  146.7 0.1 copy.35
  146.8 9.4 %all_gather.21 = bf16[64,512]{0,1:T(8,128)(2,1)S(1)} all-gather(bf16[64,64]{0,1:T(8,128)(2,1)S(1)} %copy.35), channel_id=1, replica_groups=mesh['row'=8,'col'=4] {'row'}, dimensions={1}, use_global_device_ids=true | all-gather | bytes 73728 | tf_op jit(solution)/shard_map/all_gather | solution.py:72
  156.1 0.1 copy.37
  156.2 0.8 gather_fusion.3
  157.0 1.5 fusion.33
  158.5 2.0 fusion.16
  160.5 0.7 copy.91
  161.2 0.0 reduce-scatter.15.cloned.1.call-update
  161.2 0.0 reduce-scatter.23.cloned.1.call-start
  161.2 19.3 %reduce-scatter.15.cloned.1.call-done = f32[64,128]{1,0:T(8,128)} async-done(((f32[64,512]{1,0:T(8,128)}), f32[64,128]{1,0:T(8,128)}) %reduce-scatter.15.cloned.1.call-update) | async-done | bytes 32784 | tf_op jit(solution)/shard_map/reduce_scatter | solution.py:80
  180.6 0.8 fusion.95
  181.4 12.0 %all_gather.22 = bf16[64,512]{1,0:T(8,128)(2,1)S(1)} all-gather(bf16[64,128]{1,0:T(8,128)(2,1)S(1)} %fusion.95), channel_id=1, replica_groups=mesh['row'=8,'col'=4] {'col'}, dimensions={1}, use_global_device_ids=true | all-gather | bytes 81920 | tf_op jit(solution)/shard_map/all_gather | solution.py:57
  193.4 0.7 gather_fusion.4
  194.1 0.7 fusion.36
  194.8 2.0 fusion.48
  196.8 0.8 copy.59
  197.7 0.0 reduce-scatter.17.cloned.1.call-start
  197.7 32.1 %reduce-scatter.23.cloned.1.call-done = f32[64,64]{1,0:T(8,128)} async-done(((f32[512,64]{1,0:T(8,128)}), f32[64,64]{1,0:T(8,128)}) %reduce-scatter.23.cloned.1.call-update) | async-done | bytes 16400
  229.8 0.8 copy.56
  230.6 0.7 subtract_convert_fusion
  231.3 0.1 copy.41
  231.4 9.2 %all_gather.23 = bf16[64,512]{0,1:T(8,128)(2,1)S(1)} all-gather(bf16[64,64]{0,1:T(8,128)(2,1)S(1)} %copy.41), channel_id=1, replica_groups=mesh['row'=8,'col'=4] {'row'}, dimensions={1}, use_global_device_ids=true | all-gather | bytes 73728 | tf_op jit(solution)/shard_map/all_gather | solution.py:72
  240.5 0.1 copy.43
  240.7 0.8 gather_fusion.5
  241.4 1.5 fusion.39
  243.0 2.0 fusion.12
  244.9 0.7 copy.90
  245.6 19.4 %reduce-scatter.17.cloned.1.call-done = f32[64,128]{1,0:T(8,128)} async-done(((f32[64,512]{1,0:T(8,128)}), f32[64,128]{1,0:T(8,128)}) %reduce-scatter.17.cloned.1.call-update) | async-done | bytes 32784 | tf_op jit(solution)/shard_map/reduce_scatter | solution.py:80
  265.0 1.5 multiply_reduce_fusion.2
  266.5 38.5 %all-reduce = (f32[1,64]{1,0:T(1,128)S(1)}, f32[1,64]{1,0:T(1,128)S(1)}, f32[1,64]{1,0:T(1,128)S(1)}) all-reduce(f32[1,64]{1,0:T(1,128)S(1)} %bitcast.152, f32[1,64]{1,0:T(1,128)S(1)} %bitcast.151, f32[1,64]{1,0:T(1,128)S(1)} %bitcast.150), channel_id=1, replica_groups=mesh['row'=8,'col'=4] {'row','col'}, use_global_device_ids=true, to_apply=%region_11.13 | all-reduce | flops 192 | bytes 1536 | tf_op jit(solution)/shard_map/psum | solution.py:86
  305.0 0.6 fusion.77
  (40 shorter events, 0.2 us)
Async XLA Ops:
  7.2 17.4 %copy-start = (bf16[1,1,64,128,128]{4,3,2,1,0:T(8,128)(2,1)S(1)}, bf16[1,1,64,128,128]{4,3,2,1,0:T(8,128)(2,1)}, u32[]{:S(2)}) copy-start(bf16[1,1,64,128,128]{4,3,2,1,0:T(8,128)(2,1)} %param.14) | copy-start | bytes 6291460
  7.2 54.7 %reduce-scatter.19.cloned.1.call-start = ((), (), s32[]{:S(2)}) async-start(), calls=%async_computation.9 | async-start | bytes 294912
  24.6 0.8 copy-start.9
  25.3 3.0 copy-start.11
  25.3 37.4 %copy-start.4 = (f32[64,64]{1,0:T(8,128)S(1)}, f32[64,64]{1,0:T(8,128)}, u32[]{:S(2)}) copy-start(f32[64,64]{1,0:T(8,128)} %param.18) | copy-start | bytes 49156
  25.3 37.4 %copy-start.6 = (f32[64]{0:T(128)S(1)}, f32[64]{0:T(128)}, u32[]{:S(2)}) copy-start(f32[64]{0:T(128)} %param.22) | copy-start | bytes 772
  25.3 37.4 %copy-start.7 = (f32[64]{0:T(128)S(1)}, f32[64]{0:T(128)}, u32[]{:S(2)}) copy-start(f32[64]{0:T(128)} %param.21) | copy-start | bytes 772
  25.4 37.4 %copy-start.8 = (f32[64]{0:T(128)S(1)}, f32[64]{0:T(128)}, u32[]{:S(2)}) copy-start(f32[64]{0:T(128)} %param.20) | copy-start | bytes 772
  28.2 68.3 %reduce-scatter.13.cloned.1.call-start = ((), (), s32[]{:S(2)}) async-start(), calls=%async_computation.6 | async-start | bytes 163840 | tf_op jit(solution)/shard_map/reduce_scatter | solution.py:80
  72.9 1.6 copy-start.10
  74.5 2.7 copy-start.12
  74.5 22.0 %copy-start.1 = (f32[64,128]{1,0:T(8,128)S(1)}, f32[64,128]{1,0:T(8,128)}, u32[]{:S(2)}) copy-start(f32[64,128]{1,0:T(8,128)} %param.19) | copy-start | bytes 98308
  74.5 22.0 %copy-start.2 = (f32[64,128]{1,0:T(8,128)S(1)}, f32[64,128]{1,0:T(8,128)}, u32[]{:S(2)}) copy-start(f32[64,128]{1,0:T(8,128)} %param.25) | copy-start | bytes 98308
  77.2 68.6 %reduce-scatter.21.cloned.1.call-start = ((), (), s32[]{:S(2)}) async-start(), calls=%async_computation.10 | async-start | bytes 294912
  113.6 67.0 %reduce-scatter.15.cloned.1.call-start = ((), (), s32[]{:S(2)}) async-start(), calls=%async_computation.7 | async-start | bytes 163840 | tf_op jit(solution)/shard_map/reduce_scatter | solution.py:80
  158.5 22.0 %copy-start.3 = (f32[64,128]{1,0:T(8,128)S(1)}, f32[64,128]{1,0:T(8,128)}, u32[]{:S(2)}) copy-start(f32[64,128]{1,0:T(8,128)} %reduce-scatter.13.cloned.1.call-done) | copy-start | bytes 98308
  161.2 68.6 %reduce-scatter.23.cloned.1.call-start = ((), (), s32[]{:S(2)}) async-start(), calls=%async_computation.11 | async-start | bytes 294912
  197.7 67.3 %reduce-scatter.17.cloned.1.call-start = ((), (), s32[]{:S(2)}) async-start(), calls=%async_computation.8 | async-start | bytes 163840 | tf_op jit(solution)/shard_map/reduce_scatter | solution.py:80
  243.0 22.0 %copy-start.5 = (f32[64,128]{1,0:T(8,128)S(1)}, f32[64,128]{1,0:T(8,128)}, u32[]{:S(2)}) copy-start(f32[64,128]{1,0:T(8,128)} %reduce-scatter.15.cloned.1.call-done) | copy-start | bytes 98308
Sparse Core Ops, SparseCore 0:
  28.3 33.5 reduce-scatter.18
  77.3 19.1 reduce-scatter.12
  113.7 32.0 reduce-scatter.20
  161.3 19.2 reduce-scatter.14
  197.8 31.9 reduce-scatter.22
  245.7 19.2 reduce-scatter.16
where the time goes:
time: 313 us; the launch traced here: 312 us
  waiting for transfers between devices  156 us (50%)
  blocking collectives  104 us (33%)
  matrix products  18.6 us (6%)
  between operations  15.1 us (5%)
  local copies, waits for them, and re-layouts  12.2 us (4%)
  other arithmetic  6.67 us (2%)
    unnamed x9, waiting for transfers between devices  97.9 us
    reduce_scatter x3, waiting for transfers between devices, shards(): lax.psum_scatter(partial_value, 'col', scatter_dimension=1, tiled=True)  58 us
    psum x1, blocking collectives, shards(): partial_norms.append(lax.psum(squares, ('row', 'col')))  38.5 us
    all_gather x3, blocking collectives, shards(): lax.all_gather(dual.astype(jnp.bfloat16), 'col', axis=1, tiled=True)  37.6 us
    all_gather x3, blocking collectives, shards(): gathered = lax.all_gather(extrapolated, 'row', axis=1, tiled=True)  27.7 us
    dot_general x6, matrix products, block_sum(): jnp.einsum('tr,sti->sri', onehot, product, precision=lax.Precision.HIGHEST)  11.8 us
    unnamed x35, local copies, waits for them, and re-layouts  7.05 us
  transfers between devices with their start and end apart: 6, of which 6 were waited for; matrix products, arithmetic and copies ran while one was open for 0% of the time, Pallas kernels for 0%

commit v1 on v0

v1 whole, which is shorter than its diff:
```python
import functools
import math

import jax
import jax.numpy as jnp
from jax import lax
from jax.experimental import pallas as pl
from jax.experimental.pallas import tpu as pltpu
from jax.sharding import PartitionSpec as P

ITERS = 3
PRIMAL_STEP = 0.4
DUAL_STEP = 0.4
NORM_EPS = 1e-06
MESH = pl.DeviceIdType.MESH
CHUNK = 512
VMEM_LIMIT = 56 * 1024 * 1024


def dense_kernel(rows_ref, cols_ref, count_ref, tiles_ref, hi_ref, lo_ref, acc):
    tile = tiles_ref.shape[-1]
    acc[...] = jnp.zeros_like(acc)

    def add(slot, carry):
        r = pl.multiple_of(rows_ref[0, 0, slot] * tile, tile)
        c = pl.multiple_of(cols_ref[0, 0, slot] * tile, tile)
        where = (pl.ds(r, tile), pl.ds(c, tile))
        acc[where] += tiles_ref[0, 0, slot].astype(jnp.float32)
        return carry

    lax.fori_loop(0, count_ref[0, 0], add, 0)

    def split(block, carry):
        where = (pl.ds(pl.multiple_of(block * tile, tile), tile), slice(None))
        whole = acc[where]
        hi = whole.astype(jnp.bfloat16)
        hi_ref[where] = hi
        lo_ref[where] = (whole - hi.astype(jnp.float32)).astype(jnp.bfloat16)
        return carry

    lax.fori_loop(0, acc.shape[0] // tile, split, 0)


def step_kernel(
    n_row,
    n_col,
    hi_ref,
    lo_ref,
    primal_ref,
    dual_ref,
    cost_ref,
    lower_ref,
    upper_ref,
    bound_ref,
    kind_ref,
    demand_ref,
    primal_out,
    dual_out,
    norm_out,
    duals,
    back_part,
    back_recv,
    points,
    fwd_part,
    fwd_recv,
    swap_send,
    swap_recv,
    fin_send,
    fin_recv,
    norm_row,
    norm_col,
    send_sem,
    recv_sem,
):
    me_r = lax.axis_index("row")
    me_c = lax.axis_index("col")
    block = me_r // 2
    half = lax.rem(me_r, 2)
    scen, tile = dual_ref.shape
    part = scen // 2
    width = primal_ref.shape[1]
    sibling = me_r + 1 - 2 * half

    barrier = pltpu.get_barrier_semaphore()
    for k in range(1, n_row):
        pl.semaphore_signal(
            barrier, inc=1, device_id={"row": lax.rem(me_r + k, n_row)}, device_id_type=MESH
        )
    for k in range(1, n_col):
        pl.semaphore_signal(
            barrier, inc=1, device_id={"col": lax.rem(me_c + k, n_col)}, device_id_type=MESH
        )

    def lanes(index):
        return pl.ds(pl.multiple_of(index * tile, tile), tile)

    def scens(index):
        return pl.ds(pl.multiple_of(index * part, part), part)

    def send(src, dst, sem, target):
        copy = pltpu.make_async_remote_copy(
            src_ref=src,
            dst_ref=dst,
            send_sem=send_sem.at[sem],
            recv_sem=recv_sem.at[sem],
            device_id=target,
            device_id_type=MESH,
        )
        copy.start()
        return copy

    dims = (((1,), (1,)), ((), ()))

    def multiply(left, out, flip):
        deep, wide = left.shape[1], out.shape[1]
        step, span = math.gcd(deep, CHUNK), math.gcd(wide, CHUNK)

        def term(d, w):
            x = left[:, d]
            if flip:
                return lax.dot_general(
                    x, hi_ref[w, d], dims, preferred_element_type=jnp.float32
                ) + lax.dot_general(x, lo_ref[w, d], dims, preferred_element_type=jnp.float32)
            return jnp.dot(x, hi_ref[d, w], preferred_element_type=jnp.float32) + jnp.dot(
                x, lo_ref[d, w], preferred_element_type=jnp.float32
            )

        if step == deep and span == wide:
            out[...] = term(slice(None), slice(None))
            return

        def column(j, carry):
            w = pl.ds(pl.multiple_of(j * span, span), span)

            def add(i, total):
                return total + term(pl.ds(pl.multiple_of(i * step, step), step), w)

            out[:, w] = lax.fori_loop(0, deep // step, add, jnp.zeros((scen, span), jnp.float32))
            return carry

        lax.fori_loop(0, wide // span, column, 0)

    started = []
    next_sem = [0]

    def sem():
        next_sem[0] += 1
        return next_sem[0] - 1

    def row_peer(k):
        return lax.rem(me_r + k, n_row)

    def col_peer(k):
        return lax.rem(me_c + k, n_col)

    def finish(copies):
        for copy in copies:
            copy.wait_recv()
        started.extend(copies)

    dual = dual_ref[...]
    duals[0, :, lanes(me_c)] = dual.astype(jnp.bfloat16)
    kind = bound_ref[...].reshape(1, width)
    cost_own = cost_ref[...].reshape(1, width)
    lower_own = jnp.where(kind <= 1, lower_ref[...].reshape(1, width), -jnp.inf)
    upper_own = jnp.where(kind == 0, upper_ref[...].reshape(1, width), jnp.inf)
    swap_send[...] = jnp.zeros_like(swap_send)
    swap_send[0:part, 0:width] = primal_ref[scens(1 - half), :]
    swap_send[part : part + 1, 0:width] = cost_own
    swap_send[part + 1 : part + 2, 0:width] = lower_own
    swap_send[part + 2 : part + 3, 0:width] = upper_own
    inequality = kind_ref[...].reshape(1, tile) == 1
    norm_row[me_r] = jnp.zeros(norm_row.shape[1:], jnp.float32)

    pl.semaphore_wait(barrier, n_row + n_col - 2)

    swap = None
    for it in range(ITERS):
        copies = []
        for k in range(1, n_col):
            mine = duals.at[it, :, lanes(me_c)]
            copies.append(send(mine, mine, sem(), {"col": col_peer(k)}))
        if it == 0:
            swap = send(swap_send, swap_recv, sem(), {"row": sibling})
        finish(copies)

        multiply(duals.at[it], back_part.at[it], False)
        copies = []
        for k in range(1, n_row):
            peer = row_peer(k)
            source = back_part.at[it, scens(lax.rem(peer, 2)), lanes(peer // 2)]
            copies.append(send(source, back_recv.at[it, k - 1], sem(), {"row": peer}))
        if it == 0:
            finish([swap])
            first = half == 0

            def pair(own, other):
                return jnp.where(
                    first,
                    jnp.concatenate([own, other], axis=1),
                    jnp.concatenate([other, own], axis=1),
                )

            primal = pair(primal_ref[scens(half), :], swap_recv[0:part, 0:width])
            cost = pair(cost_own, swap_recv[part : part + 1, 0:width])
            lower = pair(lower_own, swap_recv[part + 1 : part + 2, 0:width])
            upper = pair(upper_own, swap_recv[part + 2 : part + 3, 0:width])
        transposed = back_part[it, scens(half), lanes(block)]
        finish(copies)
        for k in range(1, n_row):
            transposed = transposed + back_recv[it, k - 1]

        moved = primal - PRIMAL_STEP * (cost - transposed)
        moved = jnp.minimum(jnp.maximum(moved, lower), upper)
        points[it, scens(half), lanes(block)] = (2.0 * moved - primal).astype(jnp.bfloat16)
        primal = moved
        copies = []
        for k in range(1, n_row):
            mine = points.at[it, scens(half), lanes(block)]
            copies.append(send(mine, mine, sem(), {"row": row_peer(k)}))
        last = None
        if it == ITERS - 1:
            low, high = primal[:, 0:width], primal[:, width:]
            fin_send[:, 0:width] = jnp.where(first, high, low)
            fin_send[:, width:] = jnp.zeros((part, tile - width), jnp.float32)
            last = send(fin_send, fin_recv, sem(), {"row": sibling})
            primal_out[scens(half), :] = jnp.where(first, low, high)
        finish(copies)

        multiply(points.at[it], fwd_part.at[it], True)
        copies = []
        for k in range(1, n_col):
            peer = col_peer(k)
            source = fwd_part.at[it, :, lanes(peer)]
            copies.append(send(source, fwd_recv.at[it, k - 1], sem(), {"col": peer}))
        if last is not None:
            finish([last])
            primal_out[scens(1 - half), :] = fin_recv[:, 0:width]
        image = fwd_part[it, :, lanes(me_c)]
        finish(copies)
        for k in range(1, n_col):
            image = image + fwd_recv[it, k - 1]

        gap = demand_ref[...] - image
        dual = dual + DUAL_STEP * gap
        dual = jnp.where(inequality, jnp.maximum(dual, 0.0), dual)
        if it < ITERS - 1:
            duals[it + 1, :, lanes(me_c)] = dual.astype(jnp.bfloat16)
        else:
            dual_out[...] = dual
        squares = lax.dot_general(
            jnp.ones((8, tile), jnp.float32),
            gap * gap,
            dims,
            precision=lax.Precision.HIGHEST,
            preferred_element_type=jnp.float32,
        )
        norm_row[me_r, it : it + 1, 0:scen] = squares[0:1]

    copies = []
    for k in range(1, n_row):
        mine = norm_row.at[me_r]
        copies.append(send(mine, mine, sem(), {"row": row_peer(k)}))
    finish(copies)
    total = norm_row[0]
    for r in range(1, n_row):
        total = total + norm_row[r]
    norm_col[me_c] = total
    copies = []
    for k in range(1, n_col):
        mine = norm_col.at[me_c]
        copies.append(send(mine, mine, sem(), {"col": col_peer(k)}))
    finish(copies)
    total = norm_col[0]
    for c in range(1, n_col):
        total = total + norm_col[c]
    rows = n_row * n_col * tile
    norm_out[...] = jnp.sqrt(total[0:ITERS, 0:scen] / rows + NORM_EPS)
    for copy in started:
        copy.wait_send()


def shards(
    tile_values,
    tile_row,
    tile_col,
    tile_count,
    primal_init,
    dual_init,
    cost_vector,
    lower_bound,
    upper_bound,
    bound_kind,
    row_kind,
    demand,
):
    n_row = lax.axis_size("row")
    n_col = lax.axis_size("col")
    tile = tile_values.shape[-1]
    scen, width = primal_init.shape
    part = scen // 2
    rows, cols = n_col * tile, (n_row // 2) * tile
    vmem = pl.BlockSpec(memory_space=pltpu.VMEM)
    smem = pl.BlockSpec(memory_space=pltpu.SMEM)
    half_type = jax.ShapeDtypeStruct((rows, cols), jnp.bfloat16)
    hi, lo = pl.pallas_call(
        dense_kernel,
        out_shape=(half_type, half_type),
        in_specs=[smem, smem, smem, vmem],
        out_specs=(vmem, vmem),
        scratch_shapes=[pltpu.VMEM((rows, cols), jnp.float32)],
        compiler_params=pltpu.CompilerParams(vmem_limit_bytes=VMEM_LIMIT),
    )(tile_row, tile_col, tile_count, tile_values)
    sems = ITERS * 2 * (n_row + n_col - 2) + n_row + n_col
    f32, bf16 = jnp.float32, jnp.bfloat16
    return pl.pallas_call(
        functools.partial(step_kernel, n_row, n_col),
        out_shape=(
            jax.ShapeDtypeStruct((scen, width), f32),
            jax.ShapeDtypeStruct((scen, tile), f32),
            jax.ShapeDtypeStruct((ITERS, scen), f32),
        ),
        in_specs=[vmem] * 10,
        out_specs=(vmem, vmem, vmem),
        scratch_shapes=[
            pltpu.VMEM((ITERS, scen, rows), bf16),
            pltpu.VMEM((ITERS, scen, cols), f32),
            pltpu.VMEM((ITERS, n_row - 1, part, tile), f32),
            pltpu.VMEM((ITERS, scen, cols), bf16),
            pltpu.VMEM((ITERS, scen, rows), f32),
            pltpu.VMEM((ITERS, n_col - 1, scen, tile), f32),
            pltpu.VMEM((part + 8, tile), f32),
            pltpu.VMEM((part + 8, tile), f32),
            pltpu.VMEM((part, tile), f32),
            pltpu.VMEM((part, tile), f32),
            pltpu.VMEM((n_row, 8, tile), f32),
            pltpu.VMEM((n_col, 8, tile), f32),
            pltpu.SemaphoreType.DMA((sems,)),
            pltpu.SemaphoreType.DMA((sems,)),
        ],
        compiler_params=pltpu.CompilerParams(
            collective_id=0, has_side_effects=True, vmem_limit_bytes=VMEM_LIMIT
        ),
    )(
        hi,
        lo,
        primal_init,
        dual_init,
        cost_vector,
        lower_bound,
        upper_bound,
        bound_kind,
        row_kind,
        demand,
    )


def solution(mesh):
    return jax.shard_map(
        shards,
        mesh=mesh,
        in_specs=(
            P("row", "col", None, None, None),
            P("row", "col", None),
            P("row", "col", None),
            P("row", "col"),
            P(None, ("row", "col")),
            P(None, ("row", "col")),
            P(("row", "col")),
            P(("row", "col")),
            P(("row", "col")),
            P(("row", "col")),
            P(("row", "col")),
            P(None, ("row", "col")),
        ),
        out_specs=(P(None, ("row", "col")), P(None, ("row", "col")), P()),
        check_vma=False,
    )
```

time: 313 us -> 73 us (0.23)
  waiting for transfers between devices: 156 us -> 0 us
  blocking collectives: 104 us -> 0 us
  Pallas kernels: 0 us -> 67.6 us
  matrix products: 18.6 us -> 0 us
  between operations: 15.1 us -> 1.29 us
  local copies, waits for them, and re-layouts: 12.2 us -> 3.99 us
  other arithmetic: 6.67 us -> 0 us
    unnamed x9 -> x0, waiting for transfers between devices: 97.9 us -> none
    pallas_call x0 -> x2, Pallas kernels: none -> 67.6 us  [the longest x1 64.4 us: shards(): pl.pallas_call(functools.partial(step_kernel, n_row, n_col), out_shape=(j...]
    all_gather x6 -> x0, blocking collectives: 65.3 us -> none  [the longest x3 37.6 us: shards(): lax.all_gather(dual.astype(jnp.bfloat16), 'col', axis=1, tiled=True)]
    reduce_scatter x3 -> x0, waiting for transfers between devices: 58 us -> none  [shards(): lax.psum_scatter(partial_value, 'col', scatter_dimension=1, tiled=True)]
    psum x1 -> x0, blocking collectives: 38.5 us -> none  [shards(): partial_norms.append(lax.psum(squares, ('row', 'col')))]
    dot_general x12 -> x0, matrix products: 18.6 us -> none  [the longest x6 11.8 us: block_sum(): jnp.einsum('tr,sti->sri', onehot, product, precision=lax.Precision.HIGHEST)]
    gather x6 -> x0, local copies, waits for them, and re-layouts: 4.5 us -> none  [the longest x3 2.25 us: shards(): apply_picked = jnp.take(apply_grouped, slot_cols, axis=1)]
    unnamed x35 -> x3, local copies, waits for them, and re-layouts: 7.05 us -> 3.99 us
  transfers between devices with their start and end apart: 6 -> 0, of which waited for: 6 -> 0; matrix products, arithmetic and copies ran while one was open for 0% -> 0% of each run, Pallas kernels for 0% -> 0%
where the time goes in v1:
time: 73 us; the launch traced here: 72.9 us
  Pallas kernels  67.6 us (93%)
  local copies, waits for them, and re-layouts  3.99 us (5%)
  between operations  1.29 us (2%)
    pallas_call x1, Pallas kernels, shards(): pl.pallas_call(functools.partial(step_kernel, n_row, n_col), out_shape=(j...  64.4 us
    unnamed x3, local copies, waits for them, and re-layouts  3.99 us
    pallas_call x1, Pallas kernels, shards(): pl.pallas_call(dense_kernel, out_shape=(half_type, half_type), in_specs=[...  3.16 us

profile of v1, /device:TPU:0, one launch (start us, length us, event | category | flops | bytes accessed | tf_op | source)
XLA Modules:
  0.0 72.9 jit_solution(16148653027887280877)
XLA Ops:
  1.3 3.2 %shard_map.139 = (bf16[512,512]{1,0:T(8,128)(2,1)}, bf16[512,512]{1,0:T(8,128)(2,1)}) custom-call(s32[1,1,64]{2,1,0:T(1,128)} %rows_ref.1, s32[1,1,64]{2,1,0:T(1,128)} %cols_ref.1, s32[1,1]{1,0:T(1,128)S(6)} %copy.18.count_ref, bf16[1,1,64,128,128]{4,3,2,1,0:T(8,128)(2,1)} %tiles_ref.1), custom_call_target="tpu_custom_call" | custom-call | tf_op jit(solution)/shard_map/pallas_call | solution.py:306
  4.4 64.4 %shard_map.140 = (f32[64,64]{1,0:T(8,128)}, f32[64,128]{1,0:T(8,128)}, f32[3,64]{1,0:T(4,128)}) custom-call(bf16[512,512]{1,0:T(8,128)(2,1)} %get-tuple-element.5.hi_ref, bf16[512,512]{1,0:T(8,128)(2,1)} %get-tuple-element.6.lo_ref, f32[64,64]{1,0:T(8,128)} %primal_ref.1, f32[64,128]{1,0:T(8,128)} %dual_ref.1, f32[64]{0:T(128)} %cost_ref.1, f32[64]{0:T(128)} %lower_ref.1, ...), custom_call_target="tpu_custom_call" | custom-call | tf_op jit(solution)/shard_map/pallas_call | solution.py:316
  68.9 1.4 %copy.19 = f32[64,64]{1,0:T(8,128)} copy(f32[64,64]{1,0:T(8,128)} %get-tuple-element.10) | data formatting | bytes 32768
  70.3 1.4 %copy.20 = f32[64,128]{1,0:T(8,128)} copy(f32[64,128]{1,0:T(8,128)} %get-tuple-element.11) | data formatting | bytes 65536
  71.6 1.2 %copy.21 = f32[3,64]{1,0:T(4,128)} copy(f32[3,64]{1,0:T(4,128)} %get-tuple-element.12) | data formatting | bytes 1536

commit v2 on v1

v2 whole, which is shorter than its diff:
```python
import functools
import math

import jax
import jax.numpy as jnp
from jax import lax
from jax.experimental import pallas as pl
from jax.experimental.pallas import tpu as pltpu
from jax.sharding import PartitionSpec as P

ITERS = 3
PRIMAL_STEP = 0.4
DUAL_STEP = 0.4
NORM_EPS = 1e-06
MESH = pl.DeviceIdType.MESH
CHUNK = 1024
BACK_TYPE = jnp.bfloat16
FWD_TYPE = jnp.bfloat16
VMEM_LIMIT = 56 * 1024 * 1024


def dense_kernel(rows_ref, cols_ref, count_ref, tiles_ref, hi_ref, lo_ref, acc):
    tile = tiles_ref.shape[-1]
    acc[...] = jnp.zeros_like(acc)

    def add(slot, carry):
        r = pl.multiple_of(rows_ref[0, 0, slot] * tile, tile)
        c = pl.multiple_of(cols_ref[0, 0, slot] * tile, tile)
        where = (pl.ds(r, tile), pl.ds(c, tile))
        acc[where] += tiles_ref[0, 0, slot].astype(jnp.float32)
        return carry

    lax.fori_loop(0, count_ref[0, 0], add, 0)

    def split(block, carry):
        where = (pl.ds(pl.multiple_of(block * tile, tile), tile), slice(None))
        whole = acc[where]
        hi = whole.astype(jnp.bfloat16)
        hi_ref[where] = hi
        lo_ref[where] = (whole - hi.astype(jnp.float32)).astype(jnp.bfloat16)
        return carry

    lax.fori_loop(0, acc.shape[0] // tile, split, 0)


def step_kernel(
    n_row,
    n_col,
    hi_ref,
    lo_ref,
    primal_ref,
    dual_ref,
    cost_ref,
    lower_ref,
    upper_ref,
    bound_ref,
    kind_ref,
    demand_ref,
    primal_out,
    dual_out,
    norm_out,
    full_hi,
    full_lo,
    var_send,
    var_recv,
    con_send,
    con_recv,
    dual_half,
    point,
    back_recv,
    fwd_recv,
    held,
    held_dual,
    fin_send,
    fin_recv,
    fin_dual,
    norm_row,
    local_sem,
    send_sem,
    recv_sem,
):
    me_r = lax.axis_index("row")
    me_c = lax.axis_index("col")
    chips = n_row // 2
    chip = me_r // 2
    half = lax.rem(me_r, 2)
    scen, tile = dual_ref.shape
    part = scen // 2
    width = primal_ref.shape[1]
    rows, cols = hi_ref.shape
    sibling = me_r + 1 - 2 * half

    def row_peer(k):
        return lax.rem(me_r + k, n_row)

    def col_peer(k):
        return lax.rem(me_c + k, n_col)

    barrier = pltpu.get_barrier_semaphore()
    for k in range(1, n_row):
        pl.semaphore_signal(
            barrier, inc=1, device_id={"row": row_peer(k), "col": me_c}, device_id_type=MESH
        )
    for k in range(1, n_col):
        for r in (me_r, sibling):
            pl.semaphore_signal(
                barrier, inc=1, device_id={"row": r, "col": col_peer(k)}, device_id_type=MESH
            )
    loads = [
        pltpu.make_async_copy(hi_ref, full_hi.at[0:rows], local_sem.at[0]),
        pltpu.make_async_copy(lo_ref, full_lo.at[0:rows], local_sem.at[1]),
    ]
    for load in loads:
        load.start()

    def lanes(index, offset=0):
        return pl.ds(pl.multiple_of(index * tile + offset, tile), tile)

    def scens(index):
        return pl.ds(pl.multiple_of(index * part, part), part)

    started = []
    next_sem = [0]

    def send(src, dst, r, c):
        sem = next_sem[0]
        next_sem[0] += 1
        copy = pltpu.make_async_remote_copy(
            src_ref=src,
            dst_ref=dst,
            send_sem=send_sem.at[sem],
            recv_sem=recv_sem.at[sem],
            device_id={"row": r, "col": c},
            device_id_type=MESH,
        )
        copy.start()
        return copy

    def finish(copies):
        for copy in copies:
            copy.wait_recv()
        started.extend(copies)

    dims = (((1,), (1,)), ((), ()))

    def multiply(left, out, flip):
        deep, wide = left.shape[1], out.shape[1]
        step, span = math.gcd(deep, CHUNK), math.gcd(wide, CHUNK)

        def term(d, w):
            x = left[:, d]
            if flip:
                return lax.dot_general(
                    x, full_hi[w, d], dims, preferred_element_type=jnp.float32
                ) + lax.dot_general(x, full_lo[w, d], dims, preferred_element_type=jnp.float32)
            return jnp.dot(x, full_hi[d, w], preferred_element_type=jnp.float32) + jnp.dot(
                x, full_lo[d, w], preferred_element_type=jnp.float32
            )

        if step == deep and span == wide:
            out[...] = term(slice(None), slice(None)).astype(out.dtype)
            return

        def column(j, carry):
            w = pl.ds(pl.multiple_of(j * span, span), span)

            def add(i, total):
                return total + term(pl.ds(pl.multiple_of(i * step, step), step), w)

            total = lax.fori_loop(0, deep // step, add, jnp.zeros((part, span), jnp.float32))
            out[:, w] = total.astype(out.dtype)
            return carry

        lax.fori_loop(0, wide // span, column, 0)

    def total_of(slots, it, count):
        total = slots[it, 0].astype(jnp.float32)
        for k in range(1, count):
            total = total + slots[it, k].astype(jnp.float32)
        return total

    kind = bound_ref[...].reshape(1, width)
    bounds = (
        cost_ref[...].reshape(1, width),
        jnp.where(kind <= 1, lower_ref[...].reshape(1, width), -jnp.inf),
        jnp.where(kind == 0, upper_ref[...].reshape(1, width), jnp.inf),
    )
    row_kind = jnp.broadcast_to(kind_ref[...].reshape(1, tile), (8, tile)).astype(jnp.float32)
    var_send[...] = jnp.zeros_like(var_send)
    for h in range(2):
        var_send[h, 0:part, 0:width] = primal_ref[h * part : (h + 1) * part, :]
        for place, value in enumerate(bounds):
            var_send[h, part + place : part + place + 1, 0:width] = value
        con_send[h, 0:part] = dual_ref[h * part : (h + 1) * part, :]
        con_send[h, part : 2 * part] = demand_ref[h * part : (h + 1) * part, :]
        con_send[h, 2 * part : 2 * part + 8] = row_kind
    var_recv[me_r] = var_send[half]
    con_recv[:, lanes(me_c)] = con_send[half]
    norm_row[me_r] = jnp.zeros(norm_row.shape[1:], jnp.float32)

    pl.semaphore_wait(barrier, n_row - 1 + 2 * (n_col - 1))

    blocks = [
        send(hi_ref, full_hi.at[rows : 2 * rows], sibling, me_c),
        send(lo_ref, full_lo.at[rows : 2 * rows], sibling, me_c),
    ]
    first_con = []
    for k in range(1, n_col):
        first_con.append(send(con_send.at[half], con_recv.at[:, lanes(me_c)], me_r, col_peer(k)))
    for k in range(n_col):
        first_con.append(
            send(con_send.at[1 - half], con_recv.at[:, lanes(me_c, rows)], sibling, col_peer(k))
        )
    first_var = []
    for k in range(1, n_row):
        peer = row_peer(k)
        first_var.append(send(var_send.at[lax.rem(peer, 2)], var_recv.at[me_r], peer, me_c))
    finish(first_con)
    dual = con_recv[0:part]
    demand = con_recv[part : 2 * part]
    inequality = con_recv[2 * part : 2 * part + 1] == 1.0
    for load in loads:
        load.wait()
    finish(blocks)

    for it in range(ITERS):
        dual_half[...] = dual.astype(jnp.bfloat16)
        multiply(dual_half, back_recv.at[it, chip], False)
        copies = []
        for k in range(1, chips):
            mine = back_recv.at[it, chip]
            copies.append(send(mine, mine, row_peer(2 * k), me_c))
        if it == 0:
            finish(first_var)
            state = jnp.concatenate([var_recv[r, :, 0:width] for r in range(n_row)], axis=1)
            primal = state[0:part]
            cost, lower, upper = (state[part + i : part + i + 1] for i in range(3))
        finish(copies)
        transposed = total_of(back_recv, it, chips)

        moved = primal - PRIMAL_STEP * (cost - transposed)
        moved = jnp.minimum(jnp.maximum(moved, lower), upper)
        point[...] = (2.0 * moved - primal).astype(jnp.bfloat16)
        primal = moved
        multiply(point, fwd_recv.at[it, me_c], True)
        copies = []
        for k in range(1, n_col):
            mine = fwd_recv.at[it, me_c]
            copies.append(send(mine, mine, me_r, col_peer(k)))
        if it == ITERS - 1:
            first = half == 0
            held[...] = primal
            both = held[:, lanes(chip)]
            low, high = both[:, 0:width], both[:, width:]
            fin_send[:, 0:width] = jnp.where(first, high, low)
            fin_send[:, width:] = jnp.zeros((part, tile - width), jnp.float32)
            last = send(fin_send, fin_recv, sibling, me_c)
            primal_out[scens(half), :] = jnp.where(first, low, high)
        finish(copies)
        if it == ITERS - 1:
            finish([last])
            primal_out[scens(1 - half), :] = fin_recv[:, 0:width]
        image = total_of(fwd_recv, it, n_col)

        gap = demand - image
        dual = dual + DUAL_STEP * gap
        dual = jnp.where(inequality, jnp.maximum(dual, 0.0), dual)
        squares = lax.dot_general(
            jnp.ones((8, 2 * rows), jnp.float32),
            gap * gap,
            dims,
            precision=lax.Precision.HIGHEST,
            preferred_element_type=jnp.float32,
        )
        norm_row[me_r, it : it + 1, 0:part] = squares[0:1]

    copies = []
    for k in range(1, n_row):
        mine = norm_row.at[me_r]
        copies.append(send(mine, mine, row_peer(k), me_c))
    held_dual[...] = dual
    last = send(held_dual.at[:, lanes(me_c, rows)], fin_dual, sibling, me_c)
    dual_out[scens(half), :] = held_dual[:, lanes(me_c)]
    finish([last])
    dual_out[scens(1 - half), :] = fin_dual[...]
    finish(copies)
    for h in range(2):
        total = norm_row[h]
        for r in range(h + 2, n_row, 2):
            total = total + norm_row[r]
        norm_out[:, h * part : (h + 1) * part] = jnp.sqrt(
            total[0:ITERS, 0:part] / (n_row * n_col * tile) + NORM_EPS
        )
    for copy in started:
        copy.wait_send()


def shards(
    tile_values,
    tile_row,
    tile_col,
    tile_count,
    primal_init,
    dual_init,
    cost_vector,
    lower_bound,
    upper_bound,
    bound_kind,
    row_kind,
    demand,
):
    n_row = lax.axis_size("row")
    n_col = lax.axis_size("col")
    tile = tile_values.shape[-1]
    scen, width = primal_init.shape
    part = scen // 2
    rows, cols = n_col * tile, (n_row // 2) * tile
    vmem = pl.BlockSpec(memory_space=pltpu.VMEM)
    smem = pl.BlockSpec(memory_space=pltpu.SMEM)
    hbm = pl.BlockSpec(memory_space=pl.ANY)
    half_type = jax.ShapeDtypeStruct((rows, cols), jnp.bfloat16)
    hi, lo = pl.pallas_call(
        dense_kernel,
        out_shape=(half_type, half_type),
        in_specs=[smem, smem, smem, vmem],
        out_specs=(vmem, vmem),
        scratch_shapes=[pltpu.VMEM((rows, cols), jnp.float32)],
        compiler_params=pltpu.CompilerParams(vmem_limit_bytes=VMEM_LIMIT),
    )(tile_row, tile_col, tile_count, tile_values)
    chips = n_row // 2
    sems = ITERS * (chips + n_col) + 2 * (n_row + n_col) + 8
    f32, bf16 = jnp.float32, jnp.bfloat16
    return pl.pallas_call(
        functools.partial(step_kernel, n_row, n_col),
        out_shape=(
            jax.ShapeDtypeStruct((scen, width), f32),
            jax.ShapeDtypeStruct((scen, tile), f32),
            jax.ShapeDtypeStruct((ITERS, scen), f32),
        ),
        in_specs=[hbm, hbm] + [vmem] * 8,
        out_specs=(vmem, vmem, vmem),
        scratch_shapes=[
            pltpu.VMEM((2 * rows, cols), bf16),
            pltpu.VMEM((2 * rows, cols), bf16),
            pltpu.VMEM((2, part + 8, tile), f32),
            pltpu.VMEM((n_row, part + 8, tile), f32),
            pltpu.VMEM((2, 2 * part + 8, tile), f32),
            pltpu.VMEM((2 * part + 8, 2 * rows), f32),
            pltpu.VMEM((part, 2 * rows), bf16),
            pltpu.VMEM((part, cols), bf16),
            pltpu.VMEM((ITERS, chips, part, cols), BACK_TYPE),
            pltpu.VMEM((ITERS, n_col, part, 2 * rows), FWD_TYPE),
            pltpu.VMEM((part, cols), f32),
            pltpu.VMEM((part, 2 * rows), f32),
            pltpu.VMEM((part, tile), f32),
            pltpu.VMEM((part, tile), f32),
            pltpu.VMEM((part, tile), f32),
            pltpu.VMEM((n_row, 8, tile), f32),
            pltpu.SemaphoreType.DMA((2,)),
            pltpu.SemaphoreType.DMA((sems,)),
            pltpu.SemaphoreType.DMA((sems,)),
        ],
        compiler_params=pltpu.CompilerParams(
            collective_id=0, has_side_effects=True, vmem_limit_bytes=VMEM_LIMIT
        ),
    )(
        hi,
        lo,
        primal_init,
        dual_init,
        cost_vector,
        lower_bound,
        upper_bound,
        bound_kind,
        row_kind,
        demand,
    )


def solution(mesh):
    return jax.shard_map(
        shards,
        mesh=mesh,
        in_specs=(
            P("row", "col", None, None, None),
            P("row", "col", None),
            P("row", "col", None),
            P("row", "col"),
            P(None, ("row", "col")),
            P(None, ("row", "col")),
            P(("row", "col")),
            P(("row", "col")),
            P(("row", "col")),
            P(("row", "col")),
            P(("row", "col")),
            P(None, ("row", "col")),
        ),
        out_specs=(P(None, ("row", "col")), P(None, ("row", "col")), P()),
        check_vma=False,
    )
```

time: 73 us -> 61.1 us (0.84)
  Pallas kernels: 67.6 us -> 55.3 us
    pallas_call x1, Pallas kernels: 64.4 us -> 52.2 us  [shards(): pl.pallas_call(functools.partial(step_kernel, n_row, n_col), out_shape=(j...]
where the time goes in v2:
time: 61.1 us; the launch traced here: 60.6 us
  Pallas kernels  55.3 us (91%)
  local copies, waits for them, and re-layouts  3.99 us (7%)
  between operations  1.29 us (2%)
    pallas_call x1, Pallas kernels, shards(): pl.pallas_call(functools.partial(step_kernel, n_row, n_col), out_shape=(j...  52.2 us
    unnamed x3, local copies, waits for them, and re-layouts  3.99 us
    pallas_call x1, Pallas kernels, shards(): pl.pallas_call(dense_kernel, out_shape=(half_type, half_type), in_specs=[...  3.15 us

profile of v2, /device:TPU:0, one launch (start us, length us, event | category | flops | bytes accessed | tf_op | source)
XLA Modules:
  0.0 60.6 jit_solution(3275684759471453951)
XLA Ops:
  1.3 3.1 %shard_map.139 = (bf16[512,512]{1,0:T(8,128)(2,1)}, bf16[512,512]{1,0:T(8,128)(2,1)}) custom-call(s32[1,1,64]{2,1,0:T(1,128)} %rows_ref.1, s32[1,1,64]{2,1,0:T(1,128)} %cols_ref.1, s32[1,1]{1,0:T(1,128)S(6)} %copy.18.count_ref, bf16[1,1,64,128,128]{4,3,2,1,0:T(8,128)(2,1)} %tiles_ref.1), custom_call_target="tpu_custom_call" | custom-call | tf_op jit(solution)/shard_map/pallas_call | solution.py:322
  4.4 52.2 %shard_map.140 = (f32[64,64]{1,0:T(8,128)}, f32[64,128]{1,0:T(8,128)}, f32[3,64]{1,0:T(4,128)}) custom-call(bf16[512,512]{1,0:T(8,128)(2,1)} %get-tuple-element.5.hi_ref, bf16[512,512]{1,0:T(8,128)(2,1)} %get-tuple-element.6.lo_ref, f32[64,64]{1,0:T(8,128)} %primal_ref.1, f32[64,128]{1,0:T(8,128)} %dual_ref.1, f32[64]{0:T(128)} %cost_ref.1, f32[64]{0:T(128)} %lower_ref.1, ...), custom_call_target="tpu_custom_call" | custom-call | tf_op jit(solution)/shard_map/pallas_call | solution.py:333
  56.6 1.4 %copy.19 = f32[64,64]{1,0:T(8,128)} copy(f32[64,64]{1,0:T(8,128)} %get-tuple-element.10) | data formatting | bytes 32768
  58.0 1.4 %copy.20 = f32[64,128]{1,0:T(8,128)} copy(f32[64,128]{1,0:T(8,128)} %get-tuple-element.11) | data formatting | bytes 65536
  59.4 1.2 %copy.21 = f32[3,64]{1,0:T(4,128)} copy(f32[3,64]{1,0:T(4,128)} %get-tuple-element.12) | data formatting | bytes 1536

commit v3 on v2

--- a/solution.py
+++ b/solution.py
@@ -143,18 +143,20 @@
 
     dims = (((1,), (1,)), ((), ()))
 
-    def multiply(left, out, flip):
+    def multiply(left, out, flip, base=0):
         deep, wide = left.shape[1], out.shape[1]
         step, span = math.gcd(deep, CHUNK), math.gcd(wide, CHUNK)
+        matrix_hi = full_hi.at[pl.ds(base, wide)] if flip else full_hi
+        matrix_lo = full_lo.at[pl.ds(base, wide)] if flip else full_lo
 
         def term(d, w):
             x = left[:, d]
             if flip:
                 return lax.dot_general(
-                    x, full_hi[w, d], dims, preferred_element_type=jnp.float32
-                ) + lax.dot_general(x, full_lo[w, d], dims, preferred_element_type=jnp.float32)
-            return jnp.dot(x, full_hi[d, w], preferred_element_type=jnp.float32) + jnp.dot(
-                x, full_lo[d, w], preferred_element_type=jnp.float32
+                    x, matrix_hi[w, d], dims, preferred_element_type=jnp.float32
+                ) + lax.dot_general(x, matrix_lo[w, d], dims, preferred_element_type=jnp.float32)
+            return jnp.dot(x, matrix_hi[d, w], preferred_element_type=jnp.float32) + jnp.dot(
+                x, matrix_lo[d, w], preferred_element_type=jnp.float32
             )
 
         if step == deep and span == wide:
@@ -242,11 +244,12 @@
         moved = jnp.minimum(jnp.maximum(moved, lower), upper)
         point[...] = (2.0 * moved - primal).astype(jnp.bfloat16)
         primal = moved
-        multiply(point, fwd_recv.at[it, me_c], True)
         copies = []
-        for k in range(1, n_col):
-            mine = fwd_recv.at[it, me_c]
-            copies.append(send(mine, mine, me_r, col_peer(k)))
+        for group in range(2):
+            mine = fwd_recv.at[it, me_c, :, group * rows : (group + 1) * rows]
+            multiply(point, mine, True, group * rows)
+            for k in range(1, n_col):
+                copies.append(send(mine, mine, me_r, col_peer(k)))
         if it == ITERS - 1:
             first = half == 0
             held[...] = primal
@@ -293,6 +296,12 @@
         )
     for copy in started:
         copy.wait_send()
+
+
+def tail_kernel(primal_ref, dual_ref, norm_ref, primal_out, dual_out, norm_out):
+    primal_out[...] = primal_ref[...]
+    dual_out[...] = dual_ref[...]
+    norm_out[...] = norm_ref[...]
 
 
 def shards(
@@ -328,15 +337,16 @@
         compiler_params=pltpu.CompilerParams(vmem_limit_bytes=VMEM_LIMIT),
     )(tile_row, tile_col, tile_count, tile_values)
     chips = n_row // 2
-    sems = ITERS * (chips + n_col) + 2 * (n_row + n_col) + 8
+    sems = ITERS * (chips + 2 * n_col) + 2 * (n_row + n_col) + 8
     f32, bf16 = jnp.float32, jnp.bfloat16
-    return pl.pallas_call(
+    outs = (
+        jax.ShapeDtypeStruct((scen, width), f32),
+        jax.ShapeDtypeStruct((scen, tile), f32),
+        jax.ShapeDtypeStruct((ITERS, scen), f32),
+    )
+    results = pl.pallas_call(
         functools.partial(step_kernel, n_row, n_col),
-        out_shape=(
-            jax.ShapeDtypeStruct((scen, width), f32),
-            jax.ShapeDtypeStruct((scen, tile), f32),
-            jax.ShapeDtypeStruct((ITERS, scen), f32),
-        ),
+        out_shape=outs,
         in_specs=[hbm, hbm] + [vmem] * 8,
         out_specs=(vmem, vmem, vmem),
         scratch_shapes=[
@@ -375,6 +385,9 @@
         row_kind,
         demand,
     )
+    return pl.pallas_call(
+        tail_kernel, out_shape=outs, in_specs=[vmem] * 3, out_specs=(vmem, vmem, vmem)
+    )(*results)
 
 
 def solution(mesh):

time: 61.1 us -> 58.9 us (0.964)
  local copies, waits for them, and re-layouts: 3.99 us -> 0 us
  Pallas kernels: 55.3 us -> 57.2 us
    unnamed x3 -> x0, local copies, waits for them, and re-layouts: 3.99 us -> none
    pallas_call x1 -> x2, Pallas kernels: 52.2 us -> 53.7 us  [the longest x1 52.3 us: shards(): pl.pallas_call(functools.partial(step_kernel, n_row, n_col), out_shape=ou...]
where the time goes in v3:
time: 58.9 us; the launch traced here: 58.5 us
  Pallas kernels  57.2 us (97%)
  between operations  1.29 us (2%)
    pallas_call x1, Pallas kernels, shards(): pl.pallas_call(functools.partial(step_kernel, n_row, n_col), out_shape=ou...  52.3 us
    pallas_call x1, Pallas kernels, shards(): pl.pallas_call(dense_kernel, out_shape=(half_type, half_type), in_specs=[...  3.52 us
    pallas_call x1, Pallas kernels, shards(): pl.pallas_call(tail_kernel, out_shape=outs, in_specs=[vmem] * 3, out_spec...  1.41 us

profile of v3, /device:TPU:0, one launch (start us, length us, event | category | flops | bytes accessed | tf_op | source)
XLA Modules:
  0.0 58.5 jit_solution(13959470427617548848)
XLA Ops:
  1.3 3.5 %shard_map.139 = (bf16[512,512]{1,0:T(8,128)(2,1)}, bf16[512,512]{1,0:T(8,128)(2,1)}) custom-call(s32[1,1,64]{2,1,0:T(1,128)} %rows_ref.1, s32[1,1,64]{2,1,0:T(1,128)} %cols_ref.1, s32[1,1]{1,0:T(1,128)S(6)} %copy.15.count_ref, bf16[1,1,64,128,128]{4,3,2,1,0:T(8,128)(2,1)} %tiles_ref.1), custom_call_target="tpu_custom_call" | custom-call | tf_op jit(solution)/shard_map/pallas_call | solution.py:331
  4.8 52.3 %shard_map.140 = (f32[64,64]{1,0:T(8,128)}, f32[64,128]{1,0:T(8,128)}, f32[3,64]{1,0:T(4,128)}) custom-call(bf16[512,512]{1,0:T(8,128)(2,1)} %get-tuple-element.8.hi_ref, bf16[512,512]{1,0:T(8,128)(2,1)} %get-tuple-element.9.lo_ref, f32[64,64]{1,0:T(8,128)} %primal_ref.1, f32[64,128]{1,0:T(8,128)} %dual_ref.1, f32[64]{0:T(128)} %cost_ref.1, f32[64]{0:T(128)} %lower_ref.1, ...), custom_call_target="tpu_custom_call" | custom-call | tf_op jit(solution)/shard_map/pallas_call | solution.py:347
  57.1 1.4 %shard_map.141 = (f32[64,64]{1,0:T(8,128)}, f32[64,128]{1,0:T(8,128)}, f32[3,64]{1,0:T(4,128)}) custom-call(f32[64,64]{1,0:T(8,128)} %get-tuple-element.10.primal_ref, f32[64,128]{1,0:T(8,128)} %get-tuple-element.11.dual_ref, f32[3,64]{1,0:T(4,128)} %get-tuple-element.12.norm_ref), custom_call_target="tpu_custom_call" | custom-call | tf_op jit(solution)/shard_map/pallas_call | solution.py:388

commit v4 on v3

--- a/solution.py
+++ b/solution.py
@@ -169,16 +169,16 @@
             def add(i, total):
                 return total + term(pl.ds(pl.multiple_of(i * step, step), step), w)
 
-            total = lax.fori_loop(0, deep // step, add, jnp.zeros((part, span), jnp.float32))
+            total = lax.fori_loop(0, deep // step, add, jnp.zeros((left.shape[0], span), jnp.float32))
             out[:, w] = total.astype(out.dtype)
             return carry
 
         lax.fori_loop(0, wide // span, column, 0)
 
-    def total_of(slots, it, count):
-        total = slots[it, 0].astype(jnp.float32)
+    def total_of(slots, it, count, span):
+        total = slots[it, 0, span].astype(jnp.float32)
         for k in range(1, count):
-            total = total + slots[it, k].astype(jnp.float32)
+            total = total + slots[it, k, span].astype(jnp.float32)
         return total
 
     kind = bound_ref[...].reshape(1, width)
@@ -202,10 +202,6 @@
 
     pl.semaphore_wait(barrier, n_row - 1 + 2 * (n_col - 1))
 
-    blocks = [
-        send(hi_ref, full_hi.at[rows : 2 * rows], sibling, me_c),
-        send(lo_ref, full_lo.at[rows : 2 * rows], sibling, me_c),
-    ]
     first_con = []
     for k in range(1, n_col):
         first_con.append(send(con_send.at[half], con_recv.at[:, lanes(me_c)], me_r, col_peer(k)))
@@ -213,6 +209,10 @@
         first_con.append(
             send(con_send.at[1 - half], con_recv.at[:, lanes(me_c, rows)], sibling, col_peer(k))
         )
+    blocks = [
+        send(hi_ref, full_hi.at[rows : 2 * rows], sibling, me_c),
+        send(lo_ref, full_lo.at[rows : 2 * rows], sibling, me_c),
+    ]
     first_var = []
     for k in range(1, n_row):
         peer = row_peer(k)
@@ -225,49 +225,16 @@
         load.wait()
     finish(blocks)
 
-    for it in range(ITERS):
-        dual_half[...] = dual.astype(jnp.bfloat16)
-        multiply(dual_half, back_recv.at[it, chip], False)
-        copies = []
-        for k in range(1, chips):
-            mine = back_recv.at[it, chip]
-            copies.append(send(mine, mine, row_peer(2 * k), me_c))
-        if it == 0:
-            finish(first_var)
-            state = jnp.concatenate([var_recv[r, :, 0:width] for r in range(n_row)], axis=1)
-            primal = state[0:part]
-            cost, lower, upper = (state[part + i : part + i + 1] for i in range(3))
-        finish(copies)
-        transposed = total_of(back_recv, it, chips)
-
-        moved = primal - PRIMAL_STEP * (cost - transposed)
-        moved = jnp.minimum(jnp.maximum(moved, lower), upper)
-        point[...] = (2.0 * moved - primal).astype(jnp.bfloat16)
-        primal = moved
-        copies = []
-        for group in range(2):
-            mine = fwd_recv.at[it, me_c, :, group * rows : (group + 1) * rows]
-            multiply(point, mine, True, group * rows)
-            for k in range(1, n_col):
-                copies.append(send(mine, mine, me_r, col_peer(k)))
-        if it == ITERS - 1:
-            first = half == 0
-            held[...] = primal
-            both = held[:, lanes(chip)]
-            low, high = both[:, 0:width], both[:, width:]
-            fin_send[:, 0:width] = jnp.where(first, high, low)
-            fin_send[:, width:] = jnp.zeros((part, tile - width), jnp.float32)
-            last = send(fin_send, fin_recv, sibling, me_c)
-            primal_out[scens(half), :] = jnp.where(first, low, high)
-        finish(copies)
-        if it == ITERS - 1:
-            finish([last])
-            primal_out[scens(1 - half), :] = fin_recv[:, 0:width]
-        image = total_of(fwd_recv, it, n_col)
-
-        gap = demand - image
-        dual = dual + DUAL_STEP * gap
-        dual = jnp.where(inequality, jnp.maximum(dual, 0.0), dual)
+    gaps = []
+
+    def settle(it, g):
+        gap = demand[spans[g]] - total_of(fwd_recv, it, n_col, spans[g])
+        moved = dual_parts[g] + DUAL_STEP * gap
+        dual_parts[g] = jnp.where(inequality, jnp.maximum(moved, 0.0), moved)
+        gaps.append(gap)
+
+    def square(it):
+        gap = jnp.concatenate(gaps[2 * it : 2 * it + 2], axis=0)
         squares = lax.dot_general(
             jnp.ones((8, 2 * rows), jnp.float32),
             gap * gap,
@@ -277,6 +244,55 @@
         )
         norm_row[me_r, it : it + 1, 0:part] = squares[0:1]
 
+    group = part // 2
+    spans = [slice(g * group, (g + 1) * group) for g in range(2)]
+    dual_parts = [dual[span] for span in spans]
+    primal_parts = [None, None]
+    for it in range(ITERS):
+        flights = []
+        for g, span in enumerate(spans):
+            if it > 0:
+                finish(arriving[g])
+                settle(it - 1, g)
+            dual_half[span] = dual_parts[g].astype(jnp.bfloat16)
+            mine = back_recv.at[it, chip, span]
+            multiply(dual_half.at[span], mine, False)
+            flights.append([send(mine, mine, row_peer(2 * k), me_c) for k in range(1, chips)])
+        if it == 0:
+            finish(first_var)
+            state = jnp.concatenate([var_recv[r, :, 0:width] for r in range(n_row)], axis=1)
+            primal_parts = [state[span] for span in spans]
+            cost, lower, upper = (state[part + i : part + i + 1] for i in range(3))
+        else:
+            square(it - 1)
+        arriving = []
+        for g, span in enumerate(spans):
+            finish(flights[g])
+            transposed = total_of(back_recv, it, chips, span)
+            primal = primal_parts[g]
+            moved = primal - PRIMAL_STEP * (cost - transposed)
+            moved = jnp.minimum(jnp.maximum(moved, lower), upper)
+            point[span] = (2.0 * moved - primal).astype(jnp.bfloat16)
+            primal_parts[g] = moved
+            mine = fwd_recv.at[it, me_c, span]
+            multiply(point.at[span], mine, True)
+            arriving.append([send(mine, mine, me_r, col_peer(k)) for k in range(1, n_col)])
+    first = half == 0
+    for g, span in enumerate(spans):
+        held[span] = primal_parts[g]
+    both = held[:, lanes(chip)]
+    low, high = both[:, 0:width], both[:, width:]
+    fin_send[:, 0:width] = jnp.where(first, high, low)
+    fin_send[:, width:] = jnp.zeros((part, tile - width), jnp.float32)
+    last = send(fin_send, fin_recv, sibling, me_c)
+    primal_out[scens(half), :] = jnp.where(first, low, high)
+    for g in range(2):
+        finish(arriving[g])
+        settle(ITERS - 1, g)
+    finish([last])
+    primal_out[scens(1 - half), :] = fin_recv[:, 0:width]
+    dual = jnp.concatenate(dual_parts, axis=0)
+    square(ITERS - 1)
     copies = []
     for k in range(1, n_row):
         mine = norm_row.at[me_r]
@@ -337,7 +353,7 @@
         compiler_params=pltpu.CompilerParams(vmem_limit_bytes=VMEM_LIMIT),
     )(tile_row, tile_col, tile_count, tile_values)
     chips = n_row // 2
-    sems = ITERS * (chips + 2 * n_col) + 2 * (n_row + n_col) + 8
+    sems = ITERS * 2 * (chips + n_col) + 2 * (n_row + n_col) + 8
     f32, bf16 = jnp.float32, jnp.bfloat16
     outs = (
         jax.ShapeDtypeStruct((scen, width), f32),

time: 58.9 us -> 56.1 us (0.952)
  Pallas kernels: 57.2 us -> 54.6 us
    pallas_call x1, Pallas kernels: 52.3 us -> 49.9 us  [shards(): pl.pallas_call(functools.partial(step_kernel, n_row, n_col), out_shape=ou...]
where the time goes in v4:
time: 56.1 us; the launch traced here: 55.9 us
  Pallas kernels  54.6 us (97%)
  between operations  1.29 us (2%)
    pallas_call x1, Pallas kernels, shards(): pl.pallas_call(functools.partial(step_kernel, n_row, n_col), out_shape=ou...  49.9 us
    pallas_call x1, Pallas kernels, shards(): pl.pallas_call(dense_kernel, out_shape=(half_type, half_type), in_specs=[...  3.31 us
    pallas_call x1, Pallas kernels, shards(): pl.pallas_call(tail_kernel, out_shape=outs, in_specs=[vmem] * 3, out_spec...  1.41 us

profile of v4, /device:TPU:0, one launch (start us, length us, event | category | flops | bytes accessed | tf_op | source)
XLA Modules:
  0.0 55.9 jit_solution(8176238179762856970)
XLA Ops:
  1.3 3.3 %shard_map.139 = (bf16[512,512]{1,0:T(8,128)(2,1)}, bf16[512,512]{1,0:T(8,128)(2,1)}) custom-call(s32[1,1,64]{2,1,0:T(1,128)} %rows_ref.1, s32[1,1,64]{2,1,0:T(1,128)} %cols_ref.1, s32[1,1]{1,0:T(1,128)S(6)} %copy.15.count_ref, bf16[1,1,64,128,128]{4,3,2,1,0:T(8,128)(2,1)} %tiles_ref.1), custom_call_target="tpu_custom_call" | custom-call | tf_op jit(solution)/shard_map/pallas_call | solution.py:347
  4.6 49.9 %shard_map.140 = (f32[64,64]{1,0:T(8,128)}, f32[64,128]{1,0:T(8,128)}, f32[3,64]{1,0:T(4,128)}) custom-call(bf16[512,512]{1,0:T(8,128)(2,1)} %get-tuple-element.8.hi_ref, bf16[512,512]{1,0:T(8,128)(2,1)} %get-tuple-element.9.lo_ref, f32[64,64]{1,0:T(8,128)} %primal_ref.1, f32[64,128]{1,0:T(8,128)} %dual_ref.1, f32[64]{0:T(128)} %cost_ref.1, f32[64]{0:T(128)} %lower_ref.1, ...), custom_call_target="tpu_custom_call" | custom-call | tf_op jit(solution)/shard_map/pallas_call | solution.py:363
  54.5 1.4 %shard_map.141 = (f32[64,64]{1,0:T(8,128)}, f32[64,128]{1,0:T(8,128)}, f32[3,64]{1,0:T(4,128)}) custom-call(f32[64,64]{1,0:T(8,128)} %get-tuple-element.10.primal_ref, f32[64,128]{1,0:T(8,128)} %get-tuple-element.11.dual_ref, f32[3,64]{1,0:T(4,128)} %get-tuple-element.12.norm_ref), custom_call_target="tpu_custom_call" | custom-call | tf_op jit(solution)/shard_map/pallas_call | solution.py:404
